TPU v7x, 32 devices: a whole 2x2x4 slice. The times are simulated.
32 devices in a mesh: gy: 4 (over x, core), gx: 8 (over z, y).
Axes of the slice: x: 2, y: 2, z: 4, core: 2. Of those that a mesh axis runs over, the one named last changes fastest.
Arguments:
- control: float32 [64, 512], P('gx', 'gy'), may hold values from -6 to 6
- background_std: float32 [64, 512], P('gx', 'gy'), may hold values from 0.1 to 1.9
- class_index: int32 [2, 64, 512], P(None, 'gx', 'gy'), may hold values from 0 to 23
- rate_table: float32 [2, 24], replicated
- brightness: float32 [2, 128], P(None, 'gx'), may hold values from 0 to 0.9
- circumsolar: float32 [128, 256], P('gx'), may hold values from 0 to 3
- isotropic: float32 [256], replicated, may hold values from 0.5 to 1
- horizon: float32 [256], replicated, may hold values from 0 to 1
- obs_cell: int32 [8, 4, 1024], P('gx', 'gy'), may hold values from 0 to 1023
- obs_subhour: int32 [8, 4, 1024], P('gx', 'gy'), may hold values from 0 to 127
- obs_orient: int32 [8, 4, 1024], P('gx', 'gy'), may hold values from 0 to 255
- obs_value: float32 [8, 4, 1024], P('gx', 'gy'), may hold values from -6 to 6
Outputs:
- increment: float32 [64, 512], P('gx', 'gy')
- departure: float32 [8, 4, 1024], P('gx', 'gy')
All inputs are finite; a program needn't handle non-finite values.
Results may differ from a plain program's by a relative error of at most 0.00002.
Values sent between devices are 32-bit elements; how exact they have to be, the bound alone decides.
No kernel may reach another device: no remote copies, remote signals or barrier semaphores. Data moves between devices by JAX's collectives and lax.ppermute only.
A program may use at most 64 MiB of HBM per device.

v0:
```python
import jax
import jax.numpy as jnp
from jax import lax
from jax.sharding import PartitionSpec as P


def prefix(part, axis, combine, identity, reverse):
    count = lax.axis_size(axis)
    place = lax.axis_index(axis)
    ahead = count - 1 - place if reverse else place
    gathered = jax.tree.map(lambda a: lax.all_gather(a, axis), part)
    state = jax.tree.map(lambda a, e: jnp.zeros_like(a) + jnp.asarray(e, a.dtype), part, identity)

    def one(turn, state):
        source = count - 1 - turn if reverse else turn
        return combine(
            state, jax.tree.map(lambda a: lax.dynamic_index_in_dim(a, source, 0, False), gathered)
        )

    return lax.fori_loop(0, ahead, one, state)


def lookup(rate_row, class_ids):
    result = jnp.zeros(class_ids.shape, jnp.float32)
    for class_no in range(rate_row.shape[0]):
        result = jnp.where(class_ids == class_no, rate_row[class_no], result)
    return result


def compose_link(earlier, later):
    return (earlier[0] * later[0], later[0] * earlier[1] + later[1])


def first_order(decay_rate, source, start, cell_axis, reverse):
    if cell_axis == source.ndim - 1:
        product, current = lax.associative_scan(
            compose_link, (decay_rate, source), reverse=reverse, axis=cell_axis
        )
        return current + product * start

    def advance(current, inputs):
        current = inputs[0] * current + inputs[1]
        return (current, current)

    initial = jnp.take(
        jnp.broadcast_to(jnp.asarray(start, jnp.float32), source.shape), 0, axis=cell_axis
    )
    moved_rates = jnp.moveaxis(decay_rate, cell_axis, 0)
    moved_source = jnp.moveaxis(source, cell_axis, 0)
    _, outputs = lax.scan(advance, initial, (moved_rates, moved_source), reverse=reverse)
    return jnp.moveaxis(outputs, 0, cell_axis)


def cascade(rates, source, starts, cell_axis, reverse):
    decay_rate = 1.0 - rates
    edge_index = 0 if reverse else source.shape[cell_axis] - 1
    current = source
    edge_states = []
    for section_no in range(4):
        current = first_order(decay_rate, rates * current, starts[section_no], cell_axis, reverse)
        edge_states.append(jnp.take(current, edge_index, axis=cell_axis))
    return (current, jnp.stack(edge_states))


def compose_maps(earlier, later):
    matrix = jnp.sum(later[0][:, :, None] * earlier[0][None, :, :], axis=1)
    offset_terms = jnp.sum(later[0] * earlier[1][None], axis=1) + later[1]
    return (matrix, offset_terms)


def block_maps(rates, source, cell_axis, reverse):
    zero_out, offset_terms = cascade(rates, source, [0.0, 0.0, 0.0, 0.0], cell_axis, reverse)
    identity = jnp.eye(4, dtype=jnp.float32)
    batch_shape = (4,) + source.shape
    batch_rates = jnp.broadcast_to(rates[None], batch_shape)
    batch = jnp.zeros(batch_shape, jnp.float32)
    starts = [identity[:, which].reshape(4, 1, 1) for which in range(4)]
    responses, matrix = cascade(batch_rates, batch, starts, cell_axis + 1, reverse)
    return (zero_out, responses, matrix, offset_terms)


def finish_block(zero_out, responses, incoming, cell_axis):
    result = zero_out
    for which in range(4):
        result = result + responses[which] * jnp.expand_dims(incoming[which], cell_axis)
    return result


def neutral_maps(matrix):
    identity = jnp.eye(4, dtype=jnp.float32)
    return (
        jnp.broadcast_to(identity[:, :, None], matrix.shape),
        jnp.zeros(matrix.shape[1:], jnp.float32),
    )


def x_chain(rates, source, reverse):
    zero_out, responses, matrix, offset_terms = block_maps(rates, source, 0, reverse)
    carried = prefix((matrix, offset_terms), "gx", compose_maps, neutral_maps(matrix), reverse)
    return finish_block(zero_out, responses, carried[1], 0)


def y_chain(rates, source, reverse):
    zero_out, responses, matrix, offset_terms = block_maps(rates, source, 1, reverse)
    carried = prefix((matrix, offset_terms), "gy", compose_maps, neutral_maps(matrix), reverse)
    return finish_block(zero_out, responses, carried[1], 1)


def on_device(
    control,
    background_std,
    class_index,
    rate_table,
    brightness,
    circumsolar,
    isotropic,
    horizon,
    obs_cell,
    obs_subhour,
    obs_orient,
    obs_value,
):
    rate_x = lookup(rate_table[0], class_index[0])
    rate_y = lookup(rate_table[1], class_index[1])
    perez_local = (
        (1.0 - brightness[0][:, None]) * isotropic[None, :]
        + brightness[0][:, None] * circumsolar
        + brightness[1][:, None] * horizon[None, :]
    )
    perez_table = lax.all_gather(perez_local, "gx", axis=0, tiled=True)
    spread = control * background_std * lax.rsqrt(rate_x)
    smooth_x = x_chain(rate_x, x_chain(rate_x, spread, False), True)
    scaled = smooth_x * lax.rsqrt(rate_y)
    smooth_y = y_chain(rate_y, y_chain(rate_y, scaled, False), True)
    increment = background_std * (control + smooth_y)
    orient_count = perez_table.shape[1]
    values = jnp.take(increment.reshape(-1), obs_cell.reshape(-1))
    factors = jnp.take(
        perez_table.reshape(-1), obs_subhour.reshape(-1) * orient_count + obs_orient.reshape(-1)
    )
    departure = (obs_value.reshape(-1) - factors * values).reshape(obs_value.shape)
    return (increment, departure)


def solution(mesh):
    in_specs = (
        P("gx", "gy"),
        P("gx", "gy"),
        P(None, "gx", "gy"),
        P(),
        P(None, "gx"),
        P("gx", None),
        P(),
        P(),
        P("gx", "gy", None),
        P("gx", "gy", None),
        P("gx", "gy", None),
        P("gx", "gy", None),
    )
    out_specs = (P("gx", "gy"), P("gx", "gy", None))
    return jax.shard_map(
        on_device, mesh=mesh, in_specs=in_specs, out_specs=out_specs, check_vma=False
    )
```

profile of v0, /device:TPU:0, one launch (start us, length us, event | category | flops | bytes accessed | tf_op | source)
XLA Modules:
  0.0 375.2 jit_solution(9442984984991710054)
XLA Ops:
  0.6 2.1 fusion.162
  2.7 0.7 copy-done.1
  3.4 0.7 fusion.161
  4.2 0.7 fusion.163
  4.9 0.7 copy-done.7
  5.5 15.0 %multiply_multiply_fusion = (f32[8,128]{1,0:T(8,128)S(1)}, f32[8,128]{1,0:T(8,128)S(1)}, pred[1,8,128]{2,1,0:T(8,128)(4,1)S(1)}, pred[1,8,128]{2,1,0:T(8,128)(4,...) fusion(f32[8,128]{1,0:T(8,128)S(1)} %copy-done.8, ...), kind=kLoop, calls=%fused_computation.624 | loop fusion | flops 52224 | bytes 29792 | tf_op jit(solution)/shard_map/mul | solution.py:60
  20.6 0.6 while.304
  21.2 0.6 while.305
  21.8 0.6 while.306
  22.4 0.6 while.307
  23.0 27.8 %all-gather.8 = f32[8,4,128]{2,1,0:T(4,128)S(1)} all-gather(f32[1,4,128]{2,1,0:T(4,128)S(1)} %maximum_bitcast_fusion), channel_id=3, replica_groups=mesh['gy'=4,'gx'=8] {'gx'}, dimensions={0}, use_global_device_ids=true | all-gather | bytes 18432 | tf_op jit(solution)/shard_map/all_gather | solution.py:11
  50.8 15.0 %broadcast_multiply_fusion.13 = (f32[8,128]{1,0:T(8,128)S(1)}, f32[8,128]{1,0:T(8,128)S(1)}) fusion(pred[1,8,128]{2,1,0:T(8,128)(4,1)S(1)} %get-tuple-element.1819, pred[1,8,128]{2,1,0:T(8,128)(4,1)S(1)} %get-tuple-element.1818, pred[1,8,128]{2,1,0:T(8,128)(4,1)S(1)} %get-tuple-element.1817, pred[1,8,128]{2,1,0:T(8,128)(4,1)S(1)} %get-tuple-element.1816, ...), kind=kLoop, calls=%fused_computation.654 | loop fusion | flops 40960 | bytes 21600 | tf_op jit(solution)/shard_map/mul | solution.py:60
  67.7 30.5 %all-gather = f32[32,4,128]{2,1,0:T(4,128)S(1)} all-gather(f32[4,4,128]{2,1,0:T(4,128)S(1)} %pad_maximum_fusion.60), channel_id=2, replica_groups=mesh['gy'=4,'gx'=8] {'gx'}, dimensions={0}, use_global_device_ids=true | all-gather | bytes 73728 | tf_op jit(solution)/shard_map/all_gather | solution.py:11
  98.3 0.6 while.308
  98.9 0.6 while.309
  99.5 0.6 while.310
  100.1 0.6 while.311
  100.7 26.0 %all-gather.9 = f32[8,4,128]{2,1,0:T(4,128)S(1)} all-gather(f32[1,4,128]{2,1,0:T(4,128)S(1)} %maximum_bitcast_fusion.1), channel_id=5, replica_groups=mesh['gy'=4,'gx'=8] {'gx'}, dimensions={0}, use_global_device_ids=true | all-gather | bytes 18432 | tf_op jit(solution)/shard_map/all_gather | solution.py:11
  127.5 0.5 while.300
  128.1 30.5 %all-gather.2 = f32[32,4,128]{2,1,0:T(4,128)S(1)} all-gather(f32[4,4,128]{2,1,0:T(4,128)S(1)} %pad_maximum_fusion.61), channel_id=4, replica_groups=mesh['gy'=4,'gx'=8] {'gx'}, dimensions={0}, use_global_device_ids=true | all-gather | bytes 73728 | tf_op jit(solution)/shard_map/all_gather | solution.py:11
  158.6 0.5 while.301
  159.1 14.9 %fusion.88 = (f32[8,128]{1,0:T(8,128)S(1)}, f32[8,128]{1,0:T(8,128)S(1)}, pred[1,8,128]{2,1,0:T(8,128)(4,1)S(1)}, pred[1,8,128]{2,1,0:T(8,128)(4,1)S(1)}, pred[1...) fusion(f32[4,8,128]{2,1,0:T(8,128)S(1)} %bitcast.780, ...), kind=kLoop, calls=%fused_computation.366 | loop fusion | flops 59392 | bytes 44128 | tf_op jit(solution)/shard_map/mul | solution.py:60
  192.6 5.2 %all-gather.10 = f32[4,4,8]{2,1,0:T(4,128)S(1)} all-gather(f32[1,4,8]{2,1,0:T(4,128)S(1)} %maximum_bitcast_fusion.2), channel_id=7, replica_groups=mesh['gy'=4,'gx'=8] {'gy'}, dimensions={0}, use_global_device_ids=true | all-gather | bytes 640 | tf_op jit(solution)/shard_map/all_gather | solution.py:11
  197.7 14.9 %broadcast_subtract_fusion.1 = (f32[8,128]{1,0:T(8,128)S(1)}, f32[8,128]{1,0:T(8,128)S(1)}) fusion(pred[1,8,128]{2,1,0:T(8,128)(4,1)S(1)} %get-tuple-element.1808, pred[1,8,128]{2,1,0:T(8,128)(4,1)S(1)} %get-tuple-element.1807, pred[1,8,128]{2,1,0:T(8,128)(4,1)S(1)} %get-tuple-element.1806, pred[1,8,128]{2,1,0:T(8,128)(4,1)S(1)} %get-tuple-element.1805, ...), kind=kLoop, calls=%fused_computation.649 | loop fusion | flops 40960 | bytes 21600 | tf_op jit(solution)/shard_map/sub | solution.py:55
  223.7 0.4 pad.1265
  224.2 0.5 pad.1267
  226.4 0.5 pad.1266
  227.0 0.5 pad.1253
  227.9 0.5 pad.1252
  240.4 0.5 pad.1127
  241.7 0.4 pad.1111
  242.5 0.5 pad.1126
  243.1 0.5 pad.1113
  243.8 0.5 pad.1112
  250.2 0.4 pad.1278
  251.1 0.5 pad.1281
  252.2 0.5 pad.1280
  258.5 0.4 pad.1138
  259.4 0.5 pad.1141
  260.3 0.5 pad.1140
  266.8 0.4 pad.1292
  267.6 0.5 pad.1295
  268.7 0.5 pad.1294
  273.2 0.5 pad.1148
  275.2 0.4 pad.1152
  276.1 0.5 pad.1155
  277.0 0.5 pad.1154
  283.5 0.4 pad.1306
  284.3 0.5 pad.1309
  285.5 0.5 pad.1308
  291.8 0.4 pad.1166
  292.2 0.4 pad.1167
  292.6 0.5 pad.1169
  293.6 0.5 pad.1168
  294.9 5.2 %all-gather.4 = f32[16,4,8]{2,1,0:T(4,128)S(1)} all-gather(f32[4,4,8]{2,1,0:T(4,128)S(1)} %pad_maximum_fusion.62), channel_id=6, replica_groups=mesh['gy'=4,'gx'=8] {'gy'}, dimensions={0}, use_global_device_ids=true | all-gather | bytes 2560 | tf_op jit(solution)/shard_map/all_gather | solution.py:11
  320.1 5.2 %all-gather.11 = f32[4,4,8]{2,1,0:T(4,128)S(1)} all-gather(f32[1,4,8]{2,1,0:T(4,128)S(1)} %maximum_bitcast_fusion.3), channel_id=9, replica_groups=mesh['gy'=4,'gx'=8] {'gy'}, dimensions={0}, use_global_device_ids=true | all-gather | bytes 640 | tf_op jit(solution)/shard_map/all_gather | solution.py:11
  325.7 5.2 %all-gather.6 = f32[16,4,8]{2,1,0:T(4,128)S(1)} all-gather(f32[4,4,8]{2,1,0:T(4,128)S(1)} %pad_maximum_fusion.63), channel_id=8, replica_groups=mesh['gy'=4,'gx'=8] {'gy'}, dimensions={0}, use_global_device_ids=true | all-gather | bytes 2560 | tf_op jit(solution)/shard_map/all_gather | solution.py:11
  331.2 0.6 copy-done
  331.8 4.5 %gather_fusion.1 = f32[1024]{0:T(1024)S(1)} fusion(f32[1024]{0:T(1024)S(1)} %bitcast.688, s32[1024]{0:T(1024)S(1)} %broadcast_clamp_fusion), kind=kCustom, calls=%fused_computation.1 | custom fusion | bytes 12288 | tf_op jit(solution)/shard_map/jit(_take)/gather | solution.py:137
  336.3 0.7 copy-done.12
  337.0 0.7 copy-done.10
  337.7 30.5 %all_gather.67 = f32[128,256]{1,0:T(8,128)S(1)} all-gather(f32[16,256]{1,0:T(8,128)S(1)} %multiply_add_fusion), channel_id=1, replica_groups=mesh['gy'=4,'gx'=8] {'gx'}, dimensions={0}, use_global_device_ids=true | all-gather | bytes 147456 | tf_op jit(solution)/shard_map/all_gather | solution.py:130
  368.4 6.2 %gather_fusion = f32[1024]{0:T(1024)S(1)} fusion(f32[32768]{0:T(1024)S(1)} %bitcast.689, s32[1024]{0:T(1024)S(1)} %broadcast_clamp_fusion.1), kind=kCustom, calls=%fused_computation | custom fusion | bytes 12288 | tf_op jit(solution)/shard_map/jit(_take)/gather | solution.py:138
  374.5 0.6 fusion.111
  (1459 shorter events, 110.8 us)
Async XLA Ops:
  2.7 0.7 copy-start.1
  4.1 0.7 copy-start.2
  4.1 0.7 copy-start.8
  4.8 0.7 copy-start.7
  325.7 5.5 %copy-start.5 = (s32[1,1,1024]{2,1,0:T(1,128)S(1)}, s32[1,1,1024]{2,1,0:T(1,128)}, u32[]{:S(2)}) copy-start(s32[1,1,1024]{2,1,0:T(1,128)} %param.76) | copy-start | bytes 12292
  331.2 0.6 copy-start
  331.7 5.2 %copy-start.6 = (f32[16,256]{1,0:T(8,128)S(1)}, f32[16,256]{1,0:T(8,128)}, u32[]{:S(2)}) copy-start(f32[16,256]{1,0:T(8,128)} %param.73) | copy-start | bytes 49156
  331.8 5.2 %copy-start.11 = (f32[256]{0:T(256)S(1)}, f32[256]{0:T(256)}, u32[]{:S(2)}) copy-start(f32[256]{0:T(256)} %param.74) | copy-start | bytes 3076
  336.3 0.7 copy-start.12
  337.0 0.7 copy-start.10
  337.6 30.7 %copy-start.3 = (s32[1,1,1024]{2,1,0:T(1,128)S(1)}, s32[1,1,1024]{2,1,0:T(1,128)}, u32[]{:S(2)}) copy-start(s32[1,1,1024]{2,1,0:T(1,128)} %param.78) | copy-start | bytes 12292
  337.6 30.7 %copy-start.4 = (s32[1,1,1024]{2,1,0:T(1,128)S(1)}, s32[1,1,1024]{2,1,0:T(1,128)}, u32[]{:S(2)}) copy-start(s32[1,1,1024]{2,1,0:T(1,128)} %param.77) | copy-start | bytes 12292
  368.4 6.2 %copy-start.9 = (f32[1,1,1024]{2,1,0:T(1,128)S(1)}, f32[1,1,1024]{2,1,0:T(1,128)}, u32[]{:S(2)}) copy-start(f32[1,1,1024]{2,1,0:T(1,128)} %param.79) | copy-start | bytes 12292
where the time goes:
time: 376 us; the launch traced here: 375 us
  blocking collectives  166 us (44%)
  local copies, waits for them, and re-layouts  122 us (32%)
  other arithmetic  79.3 us (21%)
  between operations  5.2 us (1%)
    all_gather x8, blocking collectives, prefix(): gathered = jax.tree.map(lambda a: lax.all_gather(a, axis), part)  136 us
    pad x240, local copies, waits for them, and re-layouts, first_order(): lax.associative_scan(compose_link, (decay_rate, source), reverse=reverse,...  53.9 us
    mul x26, other arithmetic, cascade(): rates * current  45.4 us
    slice x383, local copies, waits for them, and re-layouts, first_order(): lax.associative_scan(compose_link, (decay_rate, source), reverse=reverse,...  43.3 us
    all_gather x1, blocking collectives, on_device(): perez_table = lax.all_gather(perez_local, 'gx', axis=0, tiled=True)  30.5 us
    sub x4, other arithmetic, cascade(): decay_rate = 1.0 - rates  14.9 us
    concatenate x120, other arithmetic, first_order(): lax.associative_scan(compose_link, (decay_rate, source), reverse=reverse,...  9.28 us

commit v1 on v0

--- a/solution.py
+++ b/solution.py
@@ -2,6 +2,27 @@
 import jax.numpy as jnp
 from jax import lax
 from jax.sharding import PartitionSpec as P
+
+
+def laid_out(pieces, dim):
+    pieces = jnp.moveaxis(pieces, 0, dim)
+    dims = pieces.shape
+    return pieces.reshape(*dims[:dim], dims[dim] * dims[dim + 1], *dims[dim + 2 :])
+
+
+def doubled(array, axis):
+    size, index = (lax.axis_size(axis), lax.axis_index(axis))
+    blocks, bit = (array[None], 1)
+    while bit < size:
+        other = lax.ppermute(blocks, axis, [(i, i ^ bit) for i in range(size)])
+        low = index & bit == 0
+        blocks = jnp.concatenate([jnp.where(low, blocks, other), jnp.where(low, other, blocks)])
+        bit *= 2
+    return blocks
+
+
+def doubled_up(x, axis, dim):
+    return laid_out(doubled(x, axis), dim)
 
 
 def prefix(part, axis, combine, identity, reverse):
@@ -127,7 +148,7 @@
         + brightness[0][:, None] * circumsolar
         + brightness[1][:, None] * horizon[None, :]
     )
-    perez_table = lax.all_gather(perez_local, "gx", axis=0, tiled=True)
+    perez_table = doubled_up(perez_local, "gx", 0)
     spread = control * background_std * lax.rsqrt(rate_x)
     smooth_x = x_chain(rate_x, x_chain(rate_x, spread, False), True)
     scaled = smooth_x * lax.rsqrt(rate_y)

time: 376 us -> 352 us (0.936)
  blocking collectives: 166 us -> 134 us
  waiting for transfers between devices: 0 us -> 4.62 us
    all_gather x1 -> x0, blocking collectives: 30.5 us -> none  [on_device(): perez_table = lax.all_gather(perez_local, 'gx', axis=0, tiled=True)]
    ppermute x0 -> x3, waiting for transfers between devices: none -> 4.62 us  [doubled(): other = lax.ppermute(blocks, axis, [(i, i ^ bit) for i in range(size)])]
  transfers between devices with their start and end apart: 0 -> 3, of which waited for: 0 -> 2; matrix products, arithmetic and copies ran while one was open for 0% -> 54% of each run, Pallas kernels for 0% -> 0%
where the time goes in v1:
time: 352 us; the launch traced here: 350 us
  blocking collectives  134 us (38%)
  local copies, waits for them, and re-layouts  121 us (34%)
  other arithmetic  79.9 us (23%)
  between operations  5.16 us (1%)
  waiting for transfers between devices  4.62 us (1%)
    all_gather x8, blocking collectives, prefix(): gathered = jax.tree.map(lambda a: lax.all_gather(a, axis), part)  134 us
    pad x240, local copies, waits for them, and re-layouts, first_order(): lax.associative_scan(compose_link, (decay_rate, source), reverse=reverse,...  53.8 us
    mul x26, other arithmetic, cascade(): rates * current  45.4 us
    slice x383, local copies, waits for them, and re-layouts, first_order(): lax.associative_scan(compose_link, (decay_rate, source), reverse=reverse,...  43.6 us
    sub x4, other arithmetic, cascade(): decay_rate = 1.0 - rates  14.7 us
    concatenate x120, other arithmetic, first_order(): lax.associative_scan(compose_link, (decay_rate, source), reverse=reverse,...  9.15 us
  transfers between devices with their start and end apart: 3, of which 2 were waited for; matrix products, arithmetic and copies ran while one was open for 54% of the time, Pallas kernels for 0%

profile of v1, /device:TPU:0, one launch (start us, length us, event | category | flops | bytes accessed | tf_op | source)
XLA Modules:
  0.0 350.5 jit_solution(13662956276857928416)
XLA Ops:
  0.6 0.8 slice_bitcast_fusion.20
  1.4 0.7 copy-done.10
  2.1 0.8 add_bitcast_fusion
  2.9 3.0 collective-permute-start
  5.9 0.7 fusion.162
  6.6 0.7 fusion.161
  7.4 0.7 fusion.163
  8.1 0.7 copy-done.8
  8.8 15.1 %multiply_multiply_fusion = (f32[8,128]{1,0:T(8,128)S(1)}, f32[8,128]{1,0:T(8,128)S(1)}, pred[1,8,128]{2,1,0:T(8,128)(4,1)S(1)}, pred[1,8,128]{2,1,0:T(8,128)(4,...) fusion(f32[8,128]{1,0:T(8,128)S(1)} %copy-done.8, ...), kind=kLoop, calls=%fused_computation.633 | loop fusion | flops 52224 | bytes 29792 | tf_op jit(solution)/shard_map/mul | solution.py:81
  23.9 0.6 while.304
  24.5 0.6 while.305
  25.1 0.6 while.306
  25.8 0.6 while.307
  26.4 26.3 %all-gather.8 = f32[8,4,128]{2,1,0:T(4,128)S(1)} all-gather(f32[1,4,128]{2,1,0:T(4,128)S(1)} %maximum_bitcast_fusion), channel_id=3, replica_groups=mesh['gy'=4,'gx'=8] {'gx'}, dimensions={0}, use_global_device_ids=true | all-gather | bytes 18432 | tf_op jit(solution)/shard_map/all_gather | solution.py:32
  52.7 15.1 %broadcast_multiply_fusion.13 = (f32[8,128]{1,0:T(8,128)S(1)}, f32[8,128]{1,0:T(8,128)S(1)}) fusion(pred[1,8,128]{2,1,0:T(8,128)(4,1)S(1)} %get-tuple-element.1819, pred[1,8,128]{2,1,0:T(8,128)(4,1)S(1)} %get-tuple-element.1818, pred[1,8,128]{2,1,0:T(8,128)(4,1)S(1)} %get-tuple-element.1817, pred[1,8,128]{2,1,0:T(8,128)(4,1)S(1)} %get-tuple-element.1816, ...), kind=kLoop, calls=%fused_computation.663 | loop fusion | flops 40960 | bytes 21600 | tf_op jit(solution)/shard_map/mul | solution.py:81
  69.6 30.5 %all-gather = f32[32,4,128]{2,1,0:T(4,128)S(1)} all-gather(f32[4,4,128]{2,1,0:T(4,128)S(1)} %pad_maximum_fusion.63), channel_id=2, replica_groups=mesh['gy'=4,'gx'=8] {'gx'}, dimensions={0}, use_global_device_ids=true | all-gather | bytes 73728 | tf_op jit(solution)/shard_map/all_gather | solution.py:32
  100.2 0.6 while.308
  100.8 0.6 while.309
  101.4 0.6 while.310
  102.0 0.6 while.311
  102.6 26.0 %all-gather.9 = f32[8,4,128]{2,1,0:T(4,128)S(1)} all-gather(f32[1,4,128]{2,1,0:T(4,128)S(1)} %maximum_bitcast_fusion.1), channel_id=5, replica_groups=mesh['gy'=4,'gx'=8] {'gx'}, dimensions={0}, use_global_device_ids=true | all-gather | bytes 18432 | tf_op jit(solution)/shard_map/all_gather | solution.py:32
  129.4 0.5 while.300
  130.0 30.5 %all-gather.2 = f32[32,4,128]{2,1,0:T(4,128)S(1)} all-gather(f32[4,4,128]{2,1,0:T(4,128)S(1)} %pad_maximum_fusion.64), channel_id=4, replica_groups=mesh['gy'=4,'gx'=8] {'gx'}, dimensions={0}, use_global_device_ids=true | all-gather | bytes 73728 | tf_op jit(solution)/shard_map/all_gather | solution.py:32
  160.5 0.5 while.301
  161.0 14.7 %fusion.88 = (f32[8,128]{1,0:T(8,128)S(1)}, f32[8,128]{1,0:T(8,128)S(1)}, pred[1,8,128]{2,1,0:T(8,128)(4,1)S(1)}, pred[1,8,128]{2,1,0:T(8,128)(4,1)S(1)}, pred[1...) fusion(f32[4,8,128]{2,1,0:T(8,128)S(1)} %bitcast.784, ...), kind=kLoop, calls=%fused_computation.375 | loop fusion | flops 59392 | bytes 44128 | tf_op jit(solution)/shard_map/mul | solution.py:81
  191.7 14.7 %broadcast_subtract_fusion.1 = (f32[8,128]{1,0:T(8,128)S(1)}, f32[8,128]{1,0:T(8,128)S(1)}) fusion(pred[1,8,128]{2,1,0:T(8,128)(4,1)S(1)} %get-tuple-element.1808, pred[1,8,128]{2,1,0:T(8,128)(4,1)S(1)} %get-tuple-element.1807, pred[1,8,128]{2,1,0:T(8,128)(4,1)S(1)} %get-tuple-element.1806, pred[1,8,128]{2,1,0:T(8,128)(4,1)S(1)} %get-tuple-element.1805, ...), kind=kLoop, calls=%fused_computation.658 | loop fusion | flops 40960 | bytes 21600 | tf_op jit(solution)/shard_map/sub | solution.py:76
  222.4 0.4 pad.1265
  222.9 0.5 pad.1267
  223.9 0.4 pad.1251
  224.5 0.5 pad.1266
  225.1 0.5 pad.1253
  225.8 0.5 pad.1252
  234.2 0.4 pad.1125
  234.6 0.5 pad.1127
  235.7 0.4 pad.1111
  236.3 0.5 pad.1126
  236.9 0.5 pad.1113
  237.6 0.5 pad.1112
  248.0 0.4 pad.1279
  248.5 0.5 pad.1281
  249.1 0.5 pad.1280
  253.0 0.4 pad.1139
  253.5 0.5 pad.1141
  254.1 0.5 pad.1140
  264.6 0.4 pad.1293
  265.0 0.5 pad.1295
  265.6 0.5 pad.1294
  270.0 0.5 pad.1155
  270.7 0.8 pad.1154
  280.6 5.2 %all-gather.10 = f32[4,4,8]{2,1,0:T(4,128)S(1)} all-gather(f32[1,4,8]{2,1,0:T(4,128)S(1)} %maximum_bitcast_fusion.2), channel_id=7, replica_groups=mesh['gy'=4,'gx'=8] {'gy'}, dimensions={0}, use_global_device_ids=true | all-gather | bytes 640 | tf_op jit(solution)/shard_map/all_gather | solution.py:32
  289.6 0.5 pad.1309
  290.2 0.5 pad.1308
  294.6 0.5 pad.1169
  295.3 0.5 pad.1168
  296.5 5.2 %all-gather.4 = f32[16,4,8]{2,1,0:T(4,128)S(1)} all-gather(f32[4,4,8]{2,1,0:T(4,128)S(1)} %pad_maximum_fusion.65), channel_id=6, replica_groups=mesh['gy'=4,'gx'=8] {'gy'}, dimensions={0}, use_global_device_ids=true | all-gather | bytes 2560 | tf_op jit(solution)/shard_map/all_gather | solution.py:32
  321.7 5.2 %all-gather.11 = f32[4,4,8]{2,1,0:T(4,128)S(1)} all-gather(f32[1,4,8]{2,1,0:T(4,128)S(1)} %maximum_bitcast_fusion.3), channel_id=9, replica_groups=mesh['gy'=4,'gx'=8] {'gy'}, dimensions={0}, use_global_device_ids=true | all-gather | bytes 640 | tf_op jit(solution)/shard_map/all_gather | solution.py:32
  327.3 5.2 %all-gather.6 = f32[16,4,8]{2,1,0:T(4,128)S(1)} all-gather(f32[4,4,8]{2,1,0:T(4,128)S(1)} %pad_maximum_fusion.66), channel_id=8, replica_groups=mesh['gy'=4,'gx'=8] {'gy'}, dimensions={0}, use_global_device_ids=true | all-gather | bytes 2560 | tf_op jit(solution)/shard_map/all_gather | solution.py:32
  332.7 0.5 copy-done.5
  333.5 0.6 copy-done.6
  334.3 3.9 %collective-permute-done.1 = f32[2,16,256]{2,1,0:T(8,128)S(1)} collective-permute-done((f32[2,16,256]{2,1,0:T(8,128)S(1)}, f32[2,16,256]{2,1,0:T(8,128)S(1)}, u32[]{:S(2)}, u32[]{:S(2)}) %collective-permute-start.1) | collective-permute-done | bytes 32800 | tf_op jit(solution)/shard_map/ppermute | solution.py:17
  338.3 4.5 %gather_fusion.1 = f32[1024]{0:T(1024)S(1)} fusion(f32[1024]{0:T(1024)S(1)} %bitcast.692, s32[1024]{0:T(1024)S(1)} %broadcast_clamp_fusion), kind=kCustom, calls=%fused_computation.1 | custom fusion | bytes 12288 | tf_op jit(solution)/shard_map/jit(_take)/gather | solution.py:158
  342.8 0.7 collective-permute-done.2
  343.7 6.2 %gather_fusion = f32[1024]{0:T(1024)S(1)} fusion(f32[32768]{0:T(1024)S(1)} %bitcast.693, s32[1024]{0:T(1024)S(1)} %broadcast_clamp_fusion.1), kind=kCustom, calls=%fused_computation | custom fusion | bytes 12288 | tf_op jit(solution)/shard_map/jit(_take)/gather | solution.py:159
  349.9 0.6 fusion.111
  (1470 shorter events, 112.4 us)
Async XLA Ops:
  0.6 0.8 copy-start.12
  1.4 0.7 copy-start.10
  1.4 0.7 copy-start.9
  2.1 3.8 %copy-start.1 = (f32[2,24]{1,0:T(2,128)S(1)}, f32[2,24]{1,0:T(2,128)}, u32[]{:S(2)}) copy-start(f32[2,24]{1,0:T(2,128)} %param.71) | copy-start | bytes 580
  2.9 331.2 %collective-permute-start = (f32[1,16,256]{2,1,0:T(8,128)S(1)}, f32[1,16,256]{2,1,0:T(8,128)S(1)}, u32[]{:S(2)}, u32[]{:S(2)}) collective-permute-start(f32[1,16,256]{2,1,0:T(8,128)S(1)} %add_bitcast_fusion), channel_id=1, source_target_pairs={{0,1},{1,0},{2,3},{3,2},{4,5},{5,4},{6,7},{7,6},{8,9},{9,8},{10,11... | collective-permute-start | bytes 49160 | tf_op jit(solution)/shard_map/ppermute | solution.py:17
  8.1 0.7 copy-start.8
  8.1 0.7 copy-start.3
  8.1 0.7 copy-start.7
  332.5 0.7 copy-start.5
  332.7 0.7 copy-start.4
  333.4 0.7 copy-start.6
  333.4 0.7 copy-start.2
  334.1 4.2 %copy-start = (f32[8,128]{1,0:T(8,128)}, f32[8,128]{1,0:T(8,128)S(1)}, u32[]{:S(2)}) copy-start(f32[8,128]{1,0:T(8,128)S(1)} %fusion.69) | copy-start | bytes 12292
  334.2 4.0 %collective-permute-start.1 = (f32[2,16,256]{2,1,0:T(8,128)S(1)}, f32[2,16,256]{2,1,0:T(8,128)S(1)}, u32[]{:S(2)}, u32[]{:S(2)}) collective-permute-start(f32[2,16,256]{2,1,0:T(8,128)S(1)} %pad_maximum_fusion.2), channel_id=1, source_target_pairs={{0,2},{1,3},{2,0},{3,1},{4,6},{5,7},{6,4},{7,5},{8,10},{9,11},{10,... | collective-permute-start | bytes 98312 | tf_op jit(solution)/shard_map/ppermute | solution.py:17
  338.2 5.4 %collective-permute-start.2 = (f32[4,16,256]{2,1,0:T(8,128)S(1)}, f32[4,16,256]{2,1,0:T(8,128)S(1)}, u32[]{:S(2)}, u32[]{:S(2)}) collective-permute-start(f32[4,16,256]{2,1,0:T(8,128)S(1)} %pad_maximum_fusion.1), channel_id=1, source_target_pairs={{0,4},{1,5},{2,6},{3,7},{4,0},{5,1},{6,2},{7,3},{8,12},{9,13},{10,... | collective-permute-start | bytes 196616 | tf_op jit(solution)/shard_map/ppermute | solution.py:17
  343.7 6.2 %copy-start.11 = (f32[1,1,1024]{2,1,0:T(1,128)S(1)}, f32[1,1,1024]{2,1,0:T(1,128)}, u32[]{:S(2)}) copy-start(f32[1,1,1024]{2,1,0:T(1,128)} %param.79) | copy-start | bytes 12292
